TPU v7x, 128 devices: a whole 4x4x4 slice. The times are simulated.
128 devices in a mesh: gr: 16 (over x, y), gc: 8 (over z, core).
Axes of the slice: x: 4, y: 4, z: 4, core: 2. Of those that a mesh axis runs over, the one named last changes fastest.
Arguments:
- child_rows: float32 [8192, 12288], P('gr', 'gc'), may hold values from -1.5 to 1.5
- row_map: int32 [8192], P('gr'), may hold values from 0 to 8191, as said below
- stair: int32 [64], replicated, may hold values from 0 to 896, as said below
Outputs:
- factor: float32 [1024, 12288], P('gr', 'gc')
- projected: float32 [8192, 12288], P('gr', 'gc')
Inputs may be any that keep to these rules, and one draw needn't show every extreme that they name: row_map is a permutation of 0 to 8191. Of the 512 rows of one index of gr, at most 152 go to the rows of any one index of gr (row_map // 512), and some index of gr sends exactly 152 to one index. stair is nondecreasing and a multiple of 128; the first quarter of the blocks is 0 and the last block holds 896.
All inputs are finite; a program needn't handle non-finite values.
Results may differ from a plain program's by a relative error of at most 0.0003.
Values sent between devices are 32-bit elements; how exact they have to be, the bound alone decides.
A program may use at most 128 MiB of HBM per device.

v0:
```python
import jax
import jax.numpy as jnp
from jax import lax
from jax.sharding import PartitionSpec as P

PANEL = 512
NPANEL = 2
STAIR_BLOCK = 128


def spread(value, axis, source):
    kept = jnp.where(lax.axis_index(axis) == source, value, 0).astype(value.dtype)
    return lax.psum(kept, axis)


def pack_rows(values, targets, groups):
    rows_dev = values.shape[0]
    base_rows = 3 * rows_dev // (4 * groups)
    capacity = rows_dev - base_rows * (groups - 1)
    target_dev = targets // rows_dev
    target_row = targets % rows_dev
    onehot = (target_dev[:, None] == jnp.arange(groups, dtype=jnp.int32)[None, :]).astype(jnp.int32)
    rank_within = jnp.sum((jnp.cumsum(onehot, axis=0) - onehot) * onehot, axis=1)
    buffer_index = target_dev * capacity + rank_within
    source_row = (
        jnp.full((groups * capacity,), rows_dev, jnp.int32)
        .at[buffer_index]
        .set(jnp.arange(rows_dev, dtype=jnp.int32))
    )
    sent_rows = jnp.take(values, source_row, axis=0, mode="fill", fill_value=0.0)
    sent_slots = (
        jnp.full((groups * capacity,), rows_dev, jnp.int32).at[buffer_index].set(target_row)
    )
    return (
        sent_rows.reshape(groups, capacity, values.shape[1]),
        sent_slots.reshape(groups, capacity),
    )


def place_rows(recv_rows, recv_slots, rows_dev):
    flat_rows = recv_rows.reshape(-1, recv_rows.shape[-1])
    flat_slots = recv_slots.reshape(-1)
    where_from = (
        jnp.zeros((rows_dev,), jnp.int32)
        .at[flat_slots]
        .set(jnp.arange(flat_slots.shape[0], dtype=jnp.int32), mode="drop")
    )
    return jnp.take(flat_rows, where_from, axis=0)


def matmul(left, right):
    return jnp.dot(left, right, precision=lax.Precision.HIGHEST, preferred_element_type=jnp.float32)


def high(left, right, contract):
    return lax.dot_general(
        left,
        right,
        (contract, ((), ())),
        precision=lax.Precision.HIGH,
        preferred_element_type=jnp.float32,
    )


def inverse_factor(upper, size):
    count = upper.shape[0] // size
    eye = jnp.eye(size, dtype=upper.dtype)
    done = jnp.zeros((upper.shape[0], 0), upper.dtype)
    rest = upper
    rows = []
    for k in range(count):
        lower = lax.linalg.cholesky(rest[:size, :size], symmetrize_input=False)
        small = lax.linalg.triangular_solve(lower, eye, left_side=True, lower=True)
        scaled = matmul(small, jnp.concatenate([rest[:size, size:], done[:size]], axis=1))
        right = rest.shape[1] - size
        rows.append(
            jnp.concatenate(
                [scaled[:, right:], small, jnp.zeros((size, right), upper.dtype)], axis=1
            )
        )
        if right > 0:
            terms = jnp.concatenate([scaled, small], axis=1)
            taken = lax.dot_general(
                scaled[:, :right],
                terms,
                (((0,), (0,)), ((), ())),
                precision=lax.Precision.HIGHEST,
                preferred_element_type=jnp.float32,
            )
            rest = rest[size:, size:] - taken[:, :right]
            fresh = jnp.zeros((right, size), upper.dtype)
            done = jnp.concatenate([done[size:], fresh], axis=1) - taken[:, right:]
    return jnp.concatenate(rows, axis=0)


def shards(child_rows, row_map, stair):
    groups = lax.axis_size("gr")
    rows_dev, cols_dev = child_rows.shape
    wide = NPANEL * PANEL
    half = PANEL // 2
    columns = lax.axis_index("gc") * cols_dev + jnp.arange(cols_dev, dtype=jnp.int32)
    limits = jnp.take(stair, row_map // STAIR_BLOCK)
    masked = jnp.where(columns[None, :] >= limits[:, None], child_rows, jnp.zeros_like(child_rows))
    sent_rows, sent_slots = pack_rows(masked, row_map, groups)
    recv_slots = lax.all_to_all(sent_slots, "gr", split_axis=0, concat_axis=0, tiled=True)
    panel = spread(masked[:, :wide], "gc", 0)
    first, second = (panel[:, :PANEL], panel[:, PANEL:])
    local = high(panel, masked, ((0,), (0,)))
    top = matmul(first.T, panel)
    low = matmul(second.T, second)
    left = jnp.concatenate([top[:, :PANEL], top[:, PANEL:]], axis=0)
    low = jnp.concatenate([low[:, :half], low[:, half:]], axis=0)
    sums = lax.psum(jnp.concatenate([local, left, low], axis=1), "gr")
    sums, sent_rows = lax.optimization_barrier((sums, sent_rows))
    recv_rows = lax.all_to_all(sent_rows, "gr", split_axis=0, concat_axis=0, tiled=True)
    products = sums[:, :cols_dev]
    gram = sums[:, cols_dev:]
    low = jnp.concatenate([gram[:PANEL, PANEL:], gram[PANEL:, PANEL:]], axis=1)
    top = jnp.concatenate([gram[:PANEL, :PANEL], gram[PANEL:, :PANEL]], axis=1)
    low = jnp.concatenate([jnp.zeros_like(low), low], axis=1)
    inverse = inverse_factor(jnp.concatenate([top, low], axis=0), STAIR_BLOCK)
    front = place_rows(recv_rows, recv_slots, rows_dev)
    front_panel = spread(front[:, :wide], "gc", 0)
    basis = high(front_panel, inverse, ((1,), (1,)))
    stacked = high(inverse, products, ((1,), (0,)))
    projected = front - high(basis, stacked, ((1,), (0,)))
    share_rows = wide // groups
    factor = lax.dynamic_slice_in_dim(stacked, lax.axis_index("gr") * share_rows, share_rows, 0)
    return (factor, projected)


def solution(mesh):
    placed = (P("gr", "gc"), P("gr"), P())
    return jax.shard_map(
        shards,
        mesh=mesh,
        in_specs=placed,
        out_specs=(P("gr", "gc"), P("gr", "gc")),
        check_vma=False,
    )
```

profile of v0, /device:TPU:0, one launch (start us, length us, event | category | flops | bytes accessed | tf_op | source)
XLA Modules:
  0.0 674.6 jit_solution(3320407137401549536)
XLA Ops:
  8.8 2.1 fusion.135
  10.9 2.1 fusion.134
  13.0 2.1 fusion.136
  15.0 40.6 %select_select_fusion.8 = s32[512]{0:T(512)S(1)} fusion(s32[512]{0:T(512)} %param.7, s32[]{:T(128)} %bitcast, s32[]{:T(128)} %bitcast.1, s32[]{:T(128)} %bitcast.2, s32[]{:T(128)} %bitcast.3, s32[]{:T(128)} %bitcast.4, s32[]{:T(128)} %bitcast.5, s32[]{:T(128)} %bitcast.6, s32[]{:T(128)} %bitcast.7, s32[]{:T(128)} %bitcast.8, s32[]{:T(128)} %bitcast.9, ...), kind=kLoop, calls=%fused_computation.189 | loop fusion | flops 75776 | bytes 4352 | tf_op jit(solution)/shard_map/jit(_take)/select_n | solution.py:102
  55.7 2.2 compare_select_fusion
  59.5 68.5 %all-reduce.11.cloned.1.call-done = f32[512,1024]{1,0:T(8,128)} async-done(((f32[512,1024]{1,0:T(8,128)}), f32[512,1024]{1,0:T(8,128)}) %all-reduce.11.cloned.1.call-update) | async-done | bytes 2097168 | tf_op jit(solution)/shard_map/psum | solution.py:13
  128.0 3.5 fusion.3
  131.6 3.6 fusion.5
  135.4 5.7 fusion.138
  141.1 7.1 %maximum_maximum_fusion = f32[1024,2304]{1,0:T(8,128)} fusion(f32[512,256]{1,0:T(8,128)S(1)} %get-tuple-element.17, f32[512,256]{1,0:T(8,128)S(1)} %get-tuple-element.16, f32[512,512]{1,0:T(8,128)S(1)} %get-tuple-element.15, f32[512,512]{1,0:T(8,128)S(1)} %get-tuple-element.14, f32[1024,1536]{1,0:T(8,128)S(1)} %fusion.138), kind=kLoop, calls=%fused_computation.5 | loop fusion | flops 9437184 | bytes 18874368 | tf_op jit(solution)/shard_map/concatenate | solution.py:113
  150.4 2.5 scatter_custom_fusion.1
  153.6 6.8 %all-to-all-start = ((s32[16,1,152]{2,1,0:T(1,128)}), s32[16,1,152]{2,1,0:T(1,128)S(1)}, u32[]{:S(2)}, u32[]{:S(2)}) async-start(s32[16,1,152]{2,1,0:T(1,128)} %all_to_all.9), calls=%async_computation | async-start | bytes 32768 | tf_op jit(solution)/shard_map/all_to_all | solution.py:105
  160.5 2.5 scatter_custom_fusion
  163.1 10.0 %gather_fusion = f32[2432,1536]{1,0:T(8,128)} fusion(f32[512,1536]{1,0:T(8,128)S(1)} %compare_select_fusion, s32[3072]{0:T(1024)S(1)} %pad_clamp_fusion), kind=kCustom, calls=%fused_computation | custom fusion | bytes 29894144 | tf_op jit(solution)/shard_map/jit(_take)/gather | solution.py:30
  173.1 12.4 %broadcast_select_fusion = f32[16,152,1536]{2,1,0:T(8,128)} fusion(f32[16,152,1536]{2,1,0:T(8,128)} %bitcast.146, pred[16,152]{1,0:T(8,128)(4,1)S(1)} %broadcast_in_dim.83), kind=kLoop, calls=%fused_computation.6 | loop fusion | flops 3735552 | bytes 29886848 | tf_op jit(solution)/shard_map/jit(_take)/select_n | solution.py:30
  186.4 12.3 %scatter_custom_fusion.2 = s32[512]{0:T(512)S(1)} fusion(s32[2432]{0:T(1024)S(1)} %fusion.105, s32[2432]{0:T(1024)S(1)} %iota.147, s32[]{:T(128)} %constant.119.clone.1), kind=kCustom, calls=%fused_computation.200 | custom fusion | bytes 2052 | tf_op jit(solution)/shard_map/scatter | solution.py:46
  199.8 98.3 %all-reduce.13.cloned.1.call-done = f32[1024,2304]{1,0:T(8,128)} async-done(((f32[1024,2304]{1,0:T(8,128)}), f32[1024,2304]{1,0:T(8,128)}) %all-reduce.13.cloned.1.call-update) | async-done | bytes 9437200 | tf_op jit(solution)/shard_map/psum | solution.py:113
  300.8 5.1 all-to-all-start.1
  306.3 11.7 %custom-call.20 = f32[128,128]{1,0:T(8,128)S(1)} custom-call(f32[128,128]{1,0:T(8,128)S(1)} %slice.241), custom_call_target="Cholesky" | custom-call | tf_op jit(solution)/shard_map/cholesky/custom-call.1 | solution.py:72
  319.4 9.8 %custom-call.21 = f32[1,128,128]{1,2,0:T(8,128)S(1)} custom-call(f32[1,128,128]{2,1,0:T(8,128)S(1)} %fusion.84), custom_call_target="InvertDiagBlocksLowerTriangular" | custom-call | tf_op jit(solution)/shard_map/triangular_solve/custom-call.0 | solution.py:73
  330.0 3.1 fusion.7
  336.6 11.9 %custom-call.22 = f32[128,128]{1,0:T(8,128)S(1)} custom-call(f32[128,128]{1,0:T(8,128)S(1)} %slice.384), custom_call_target="Cholesky" | custom-call | tf_op jit(solution)/shard_map/cholesky/custom-call.1 | solution.py:72
  349.8 9.8 %custom-call.23 = f32[1,128,128]{1,2,0:T(8,128)S(1)} custom-call(f32[1,128,128]{2,1,0:T(8,128)S(1)} %fusion.85), custom_call_target="InvertDiagBlocksLowerTriangular" | custom-call | tf_op jit(solution)/shard_map/triangular_solve/custom-call.0 | solution.py:73
  361.7 2.7 fusion.11
  367.2 11.9 %custom-call.24 = f32[128,128]{1,0:T(8,128)S(1)} custom-call(f32[128,128]{1,0:T(8,128)S(1)} %slice.392), custom_call_target="Cholesky" | custom-call | tf_op jit(solution)/shard_map/cholesky/custom-call.1 | solution.py:72
  380.5 9.8 %custom-call.25 = f32[1,128,128]{1,2,0:T(8,128)S(1)} custom-call(f32[1,128,128]{2,1,0:T(8,128)S(1)} %fusion.86), custom_call_target="InvertDiagBlocksLowerTriangular" | custom-call | tf_op jit(solution)/shard_map/triangular_solve/custom-call.0 | solution.py:73
  391.9 2.3 fusion.15
  395.3 11.7 %custom-call.26 = f32[128,128]{1,0:T(8,128)S(1)} custom-call(f32[128,128]{1,0:T(8,128)S(1)} %slice.401), custom_call_target="Cholesky" | custom-call | tf_op jit(solution)/shard_map/cholesky/custom-call.1 | solution.py:72
  408.4 9.8 %custom-call.27 = f32[1,128,128]{1,2,0:T(8,128)S(1)} custom-call(f32[1,128,128]{2,1,0:T(8,128)S(1)} %fusion.87), custom_call_target="InvertDiagBlocksLowerTriangular" | custom-call | tf_op jit(solution)/shard_map/triangular_solve/custom-call.0 | solution.py:73
  420.3 1.8 fusion.19
  422.6 11.7 %custom-call.28 = f32[128,128]{1,0:T(8,128)S(1)} custom-call(f32[128,128]{1,0:T(8,128)S(1)} %slice.410), custom_call_target="Cholesky" | custom-call | tf_op jit(solution)/shard_map/cholesky/custom-call.1 | solution.py:72
  435.6 9.8 %custom-call.29 = f32[1,128,128]{1,2,0:T(8,128)S(1)} custom-call(f32[1,128,128]{2,1,0:T(8,128)S(1)} %fusion.88), custom_call_target="InvertDiagBlocksLowerTriangular" | custom-call | tf_op jit(solution)/shard_map/triangular_solve/custom-call.0 | solution.py:73
  448.2 11.9 %custom-call.30 = f32[128,128]{1,0:T(8,128)S(1)} custom-call(f32[128,128]{1,0:T(8,128)S(1)} %slice.419), custom_call_target="Cholesky" | custom-call | tf_op jit(solution)/shard_map/cholesky/custom-call.1 | solution.py:72
  461.5 9.8 %custom-call.31 = f32[1,128,128]{1,2,0:T(8,128)S(1)} custom-call(f32[1,128,128]{2,1,0:T(8,128)S(1)} %fusion.89), custom_call_target="InvertDiagBlocksLowerTriangular" | custom-call | tf_op jit(solution)/shard_map/triangular_solve/custom-call.0 | solution.py:73
  474.0 11.7 %custom-call.32 = f32[128,128]{1,0:T(8,128)S(1)} custom-call(f32[128,128]{1,0:T(8,128)S(1)} %get-tuple-element.21), custom_call_target="Cholesky" | custom-call | tf_op jit(solution)/shard_map/cholesky/custom-call.1 | solution.py:72
  487.0 10.0 %custom-call.33 = f32[1,128,128]{1,2,0:T(8,128)S(1)} custom-call(f32[1,128,128]{2,1,0:T(8,128)S(1)} %fusion.90), custom_call_target="InvertDiagBlocksLowerTriangular" | custom-call | tf_op jit(solution)/shard_map/triangular_solve/custom-call.0 | solution.py:73
  500.9 11.7 %custom-call.34 = f32[128,128]{1,0:T(8,128)S(1)} custom-call(f32[128,128]{1,0:T(8,128)S(1)} %slice_subtract_fusion.14), custom_call_target="Cholesky" | custom-call | tf_op jit(solution)/shard_map/cholesky/custom-call.1 | solution.py:72
  514.0 9.8 %custom-call.35 = f32[1,128,128]{1,2,0:T(8,128)S(1)} custom-call(f32[1,128,128]{2,1,0:T(8,128)S(1)} %fusion.91), custom_call_target="InvertDiagBlocksLowerTriangular" | custom-call | tf_op jit(solution)/shard_map/triangular_solve/custom-call.0 | solution.py:73
  525.9 1.8 maximum_dynamic-update-slice_fusion.5
  527.7 1.8 maximum_dynamic-update-slice_fusion.4
  533.5 31.4 %all-to-all-done.1 = f32[16,152,1536]{2,1,0:T(8,128)} async-done(((f32[16,152,1536]{2,1,0:T(8,128)}), f32[16,152,1536]{2,1,0:T(8,128)}, u32[]{:S(2)}, u32[]{:S(2)}) %all-to-all-start.1) | async-done | bytes 14942240 | tf_op jit(solution)/shard_map/all_to_all | solution.py:115
  564.9 10.0 %gather_fusion.1 = f32[512,1536]{1,0:T(8,128)} fusion(f32[2432,1536]{1,0:T(8,128)} %bitcast.83, s32[1024]{0:T(1024)S(1)} %copy-done.27), kind=kCustom, calls=%fused_computation.1 | custom fusion | bytes 6293504 | tf_op jit(solution)/shard_map/jit(_take)/gather | solution.py:48
  575.0 2.2 broadcast_select_fusion.1
  578.7 13.7 %fusion = f32[1024,1536]{1,0:T(8,128)S(1)} fusion(f32[1024,1024]{1,0:T(8,128)} %maximum_dynamic-update-slice_fusion, f32[1024,2304]{1,0:T(8,128)} %all-reduce.13.cloned.1.call-done), kind=kOutput, calls=%fused_computation.7 | convolution fusion | flops 9663676416 | bytes 16777216 | tf_op jit(solution)/shard_map/dot_general | solution.py:56
  592.4 2.7 copy-done.7
  595.8 57.7 %all-reduce.15.cloned.1.call-done = f32[512,1024]{1,0:T(8,128)} async-done(((f32[512,1024]{1,0:T(8,128)}), f32[512,1024]{1,0:T(8,128)}) %all-reduce.15.cloned.1.call-update) | async-done | bytes 2097168 | tf_op jit(solution)/shard_map/psum | solution.py:13
  653.5 6.8 %fusion.139 = f32[512,1024]{1,0:T(8,128)S(1)} fusion(f32[512,1024]{1,0:T(8,128)} %all-reduce.15.cloned.1.call-done, f32[1024,1024]{1,0:T(8,128)} %maximum_dynamic-update-slice_fusion), kind=kOutput, calls=%fused_computation.230 | convolution fusion | flops 3221225472 | bytes 8388608 | tf_op jit(solution)/shard_map/dot_general | solution.py:56
  660.3 7.3 %convolution_subtract_fusion = f32[512,1536]{1,0:T(8,128)} fusion(f32[512,1536]{1,0:T(8,128)S(1)} %broadcast_select_fusion.1, f32[512,1024]{1,0:T(8,128)S(1)} %fusion.139, f32[1024,1536]{1,0:T(8,128)S(1)} %copy-done.8), kind=kOutput, calls=%fused_computation.14 | convolution fusion | flops 4832624640 | bytes 14680064 | tf_op jit(solution)/shard_map/dot_general | solution.py:56
  (209 shorter events, 53.9 us)
Async XLA Ops:
  7.2 120.8 %all-reduce.11.cloned.1.call-start = ((), (), s32[]{:S(2)}) async-start(), calls=%async_computation.2 | async-start | bytes 4194304 | tf_op jit(solution)/shard_map/psum | solution.py:13
  59.4 238.8 %all-reduce.13.cloned.1.call-start = ((), (), s32[]{:S(2)}) async-start(), calls=%async_computation.3 | async-start | bytes 18874368 | tf_op jit(solution)/shard_map/psum | solution.py:113
  128.0 3.6 copy-start
  148.2 0.7 copy-start.28
  153.6 32.5 %all-to-all-start = ((s32[16,1,152]{2,1,0:T(1,128)}), s32[16,1,152]{2,1,0:T(1,128)S(1)}, u32[]{:S(2)}, u32[]{:S(2)}) async-start(s32[16,1,152]{2,1,0:T(1,128)} %all_to_all.9), calls=%async_computation | async-start | bytes 32768 | tf_op jit(solution)/shard_map/all_to_all | solution.py:105
  300.7 28.8 %copy-start.1 = (f32[512,512]{1,0:T(8,128)}, f32[512,512]{1,0:T(8,128)S(1)}, u32[]{:S(2)}) copy-start(f32[512,512]{1,0:T(8,128)S(1)} %get-tuple-element.10) | copy-start | bytes 3145732
  300.7 28.8 %copy-start.3 = (f32[512,512]{1,0:T(8,128)}, f32[512,512]{1,0:T(8,128)S(1)}, u32[]{:S(2)}) copy-start(f32[512,512]{1,0:T(8,128)S(1)} %get-tuple-element.11) | copy-start | bytes 3145732
  300.8 264.2 %all-to-all-start.1 = ((f32[16,152,1536]{2,1,0:T(8,128)}), f32[16,152,1536]{2,1,0:T(8,128)}, u32[]{:S(2)}, u32[]{:S(2)}) async-start(f32[16,152,1536]{2,1,0:T(8,128)} %broadcast_select_fusion), calls=%async_computation.1 | async-start | bytes 29884416 | tf_op jit(solution)/shard_map/all_to_all | solution.py:115
  305.9 347.7 %all-reduce.15.cloned.1.call-start = ((), (), s32[]{:S(2)}) async-start(), calls=%async_computation.4 | async-start | bytes 4194304 | tf_op jit(solution)/shard_map/psum | solution.py:13
  333.1 2.3 copy-start.2
  333.1 2.3 copy-start.4
  360.0 4.5 copy-start.15
  360.0 4.3 copy-start.14
  361.7 2.9 copy-start.11
  365.8 1.4 copy-start.5
  365.8 28.4 %copy-start.10 = (f32[640,256]{1,0:T(8,128)S(1)}, f32[640,256]{1,0:T(8,128)}, u32[]{:S(2)}) copy-start(f32[640,256]{1,0:T(8,128)} %slice.403) | copy-start | bytes 1966084
  390.7 3.7 copy-start.21
  391.9 2.5 copy-start.6
  394.3 1.0 copy-start.9
  395.3 26.8 %slice-start = ((f32[640,384]{1,0:T(8,128)}), f32[512,384]{1,0:T(8,128)S(1)}, s32[]{:S(2)}) async-start(f32[640,384]{1,0:T(8,128)} %copy-done.9), calls=%async_computation.5 | async-start | bytes 1572864 | tf_op jit(solution)/shard_map/slice | solution.py:92
  418.6 1.7 copy-start.19
  445.8 0.6 copy-start.23
  446.4 1.7 copy-start.12
  471.7 25.6 %copy-start.17 = (f32[128,128]{1,0:T(8,128)}, f32[128,128]{1,0:T(8,128)S(1)}, u32[]{:S(2)}) copy-start(f32[128,128]{1,0:T(8,128)S(1)} %copy.27) | copy-start | bytes 196612
  472.3 25.8 %copy-start.13 = (f32[128,896]{1,0:T(8,128)}, f32[128,896]{1,0:T(8,128)S(1)}, u32[]{:S(2)}) copy-start(f32[128,896]{1,0:T(8,128)S(1)} %fusion.54) | copy-start | bytes 1376260
  497.3 0.6 copy-start.25
  497.9 0.8 copy-start.26
  497.9 27.1 %slice-start.1 = ((f32[128,896]{1,0:T(8,128)}), f32[128,128]{1,0:T(8,128)S(1)}, s32[]{:S(2)}) async-start(f32[128,896]{1,0:T(8,128)} %copy-done.11), calls=%async_computation.6 | async-start | bytes 131072 | tf_op jit(solution)/shard_map/slice | solution.py:78
  497.9 27.1 %copy-start.16 = (f32[128,128]{1,0:T(8,128)S(1)}, f32[128,128]{1,0:T(8,128)}, u32[]{:S(2)}) copy-start(f32[128,128]{1,0:T(8,128)} %copy-done.15) | copy-start | bytes 196612
  498.0 27.9 %copy-start.22 = (f32[128,128]{1,0:T(8,128)S(1)}, f32[128,128]{1,0:T(8,128)}, u32[]{:S(2)}) copy-start(f32[128,128]{1,0:T(8,128)} %copy-done.21) | copy-start | bytes 196612
  498.0 29.7 %copy-start.20 = (f32[128,128]{1,0:T(8,128)S(1)}, f32[128,128]{1,0:T(8,128)}, u32[]{:S(2)}) copy-start(f32[128,128]{1,0:T(8,128)} %copy-done.19) | copy-start | bytes 196612
  498.1 31.4 %slice-start.2 = ((f32[128,896]{1,0:T(8,128)}), f32[128,512]{1,0:T(8,128)S(1)}, s32[]{:S(2)}) async-start(f32[128,896]{1,0:T(8,128)} %copy-done.12), calls=%async_computation.7 | async-start | bytes 524288 | tf_op jit(solution)/shard_map/slice | solution.py:78
  498.1 31.4 %copy-start.24 = (f32[128,128]{1,0:T(8,128)S(1)}, f32[128,128]{1,0:T(8,128)}, u32[]{:S(2)}) copy-start(f32[128,128]{1,0:T(8,128)} %copy-done.23) | copy-start | bytes 196612
  498.7 31.6 %slice-start.3 = ((f32[128,896]{1,0:T(8,128)}), f32[128,640]{1,0:T(8,128)S(1)}, s32[]{:S(2)}) async-start(f32[128,896]{1,0:T(8,128)} %copy-done.13), calls=%async_computation.8 | async-start | bytes 655360 | tf_op jit(solution)/shard_map/slice | solution.py:78
  498.7 31.6 %copy-start.18 = (f32[128,128]{1,0:T(8,128)S(1)}, f32[128,128]{1,0:T(8,128)}, u32[]{:S(2)}) copy-start(f32[128,128]{1,0:T(8,128)} %copy-done.17) | copy-start | bytes 196612
  527.7 37.2 %copy-start.27 = (s32[1024]{0:T(1024)S(1)}, s32[1024]{0:T(1024)}, u32[]{:S(2)}) copy-start(s32[1024]{0:T(1024)} %pad_clamp_fusion.1) | copy-start | bytes 12292
  564.9 10.0 %copy-start.29 = (pred[512]{0:T(512)(128)(4,1)S(1)}, pred[512]{0:T(512)(128)(4,1)}, u32[]{:S(2)}) copy-start(pred[512]{0:T(512)(128)(4,1)} %compare_and_fusion.1) | copy-start | bytes 1540
  592.4 2.7 copy-start.7
  653.5 6.8 %copy-start.8 = (f32[1024,1536]{1,0:T(8,128)S(1)}, f32[1024,1536]{1,0:T(8,128)}, u32[]{:S(2)}) copy-start(f32[1024,1536]{1,0:T(8,128)} %copy-done.7) | copy-start | bytes 18874372
Sparse Core Ops, SparseCore 0:
  59.5 68.3 all-reduce.10
  148.4 149.7 all-reduce.12
  578.8 74.6 all-reduce.14
where the time goes:
time: 685 us; the launch traced here: 675 us
  other arithmetic  264 us (39%)
  waiting for transfers between devices  256 us (37%)
  local copies, waits for them, and re-layouts  64.7 us (9%)
  matrix products  62.4 us (9%)
  between operations  15.4 us (2%)
  starting transfers between devices  12.4 us (2%)
    psum x2, waiting for transfers between devices, spread(): return lax.psum(kept, axis)  126 us
    another operation x24, other arithmetic, inverse_factor(): lower = lax.linalg.cholesky(rest[:size, :size], symmetrize_input=False)  99.8 us
    psum x1, waiting for transfers between devices, shards(): sums = lax.psum(jnp.concatenate([local, left, low], axis=1), 'gr')  98.3 us
    another operation x16, other arithmetic, inverse_factor(): small = lax.linalg.triangular_solve(lower, eye, left_side=True, lower=True)  83.9 us
    select_n x1, other arithmetic, shards(): limits = jnp.take(stair, row_map // STAIR_BLOCK)  40.6 us
    dot_general x4, matrix products, high(): lax.dot_general(left, right, (contract, ((), ())), precision=lax.Precisio...  33.4 us
    all_to_all x1, waiting for transfers between devices, shards(): lax.all_to_all(sent_rows, 'gr', split_axis=0, concat_axis=0, tiled=True)  31.4 us
    dot_general x10, matrix products, matmul(): jnp.dot(left, right, precision=lax.Precision.HIGHEST, preferred_element_t...  14 us
  transfers between devices with their start and end apart: 5, of which 4 were waited for; matrix products, arithmetic and copies ran while one was open for 42% of the time, Pallas kernels for 0%

commit v1 on v0

--- a/solution.py
+++ b/solution.py
@@ -10,7 +10,7 @@
 
 def spread(value, axis, source):
     kept = jnp.where(lax.axis_index(axis) == source, value, 0).astype(value.dtype)
-    return lax.psum(kept, axis)
+    return jnp.sum(jax.lax.all_gather(kept, axis), axis=0)
 
 
 def pack_rows(values, targets, groups):

time: 685 us -> 956 us (1.40)
  the two profiles are of different devices: /device:TPU:0 before, /device:TPU:20 now
where the time goes in v1:
time: 956 us; the launch traced here: 943 us
  waiting for transfers between devices  452 us (47%)
  other arithmetic  305 us (32%)
  local copies, waits for them, and re-layouts  81.6 us (9%)
  matrix products  75 us (8%)
  between operations  15.4 us (2%)
  starting transfers between devices  15 us (2%)
    all_to_all x1, waiting for transfers between devices, shards(): lax.all_to_all(sent_rows, 'gr', split_axis=0, concat_axis=0, tiled=True)  254 us
    psum x1, waiting for transfers between devices, shards(): sums = lax.psum(jnp.concatenate([local, left, low], axis=1), 'gr')  111 us
    another operation x24, other arithmetic, inverse_factor(): lower = lax.linalg.cholesky(rest[:size, :size], symmetrize_input=False)  110 us
    another operation x16, other arithmetic, inverse_factor(): small = lax.linalg.triangular_solve(lower, eye, left_side=True, lower=True)  97.8 us
    all_gather x2, waiting for transfers between devices, spread(): return jnp.sum(jax.lax.all_gather(kept, axis), axis=0)  87.4 us
    select_n x1, other arithmetic, shards(): limits = jnp.take(stair, row_map // STAIR_BLOCK)  40.6 us
    dot_general x4, matrix products, high(): lax.dot_general(left, right, (contract, ((), ())), precision=lax.Precisio...  33.7 us
  transfers between devices with their start and end apart: 5, of which 3 were waited for; matrix products, arithmetic and copies ran while one was open for 35% of the time, Pallas kernels for 0%

profile of v1, /device:TPU:20, one launch (start us, length us, event | category | flops | bytes accessed | tf_op | source)
XLA Modules:
  0.0 943.4 jit_solution(2402295190747168783)
XLA Ops:
  8.8 2.1 fusion.135
  10.9 2.1 fusion.134
  15.0 40.6 %select_select_fusion.8 = s32[512]{0:T(512)S(1)} fusion(s32[512]{0:T(512)} %param.7, s32[]{:T(128)} %bitcast, s32[]{:T(128)} %bitcast.1, s32[]{:T(128)} %bitcast.2, s32[]{:T(128)} %bitcast.3, s32[]{:T(128)} %bitcast.4, s32[]{:T(128)} %bitcast.5, s32[]{:T(128)} %bitcast.6, s32[]{:T(128)} %bitcast.7, s32[]{:T(128)} %bitcast.8, s32[]{:T(128)} %bitcast.9, ...), kind=kLoop, calls=%fused_computation.189 | loop fusion | flops 75776 | bytes 4352 | tf_op jit(solution)/shard_map/jit(_take)/select_n | solution.py:102
  55.7 2.2 compare_select_fusion
  59.5 87.4 %all-gather.5.cloned.1.call-done = f32[4096,1024]{1,0:T(8,128)} async-done(((f32[512,1024]{1,0:T(8,128)}), f32[4096,1024]{1,0:T(8,128)}) %all-gather.5.cloned.1.call-update) | async-done | bytes 16777232 | tf_op jit(solution)/shard_map/all_gather | solution.py:13
  146.9 9.3 reduce_sum.27
  156.2 3.6 fusion.3
  159.8 3.6 fusion.5
  163.4 5.9 fusion.138
  169.6 6.9 maximum_maximum_fusion
  178.8 2.5 scatter_custom_fusion.1
  181.9 7.2 all-to-all-start
  189.2 2.5 scatter_custom_fusion
  191.8 10.1 %gather_fusion = f32[2432,1536]{1,0:T(8,128)} fusion(f32[512,1536]{1,0:T(8,128)S(1)} %compare_select_fusion, s32[3072]{0:T(1024)S(1)} %pad_clamp_fusion), kind=kCustom, calls=%fused_computation | custom fusion | bytes 29894144 | tf_op jit(solution)/shard_map/jit(_take)/gather | solution.py:30
  201.9 12.7 %broadcast_select_fusion = f32[16,152,1536]{2,1,0:T(8,128)} fusion(f32[16,152,1536]{2,1,0:T(8,128)} %bitcast.148, pred[16,152]{1,0:T(8,128)(4,1)S(1)} %broadcast_in_dim.83), kind=kLoop, calls=%fused_computation.6 | loop fusion | flops 3735552 | bytes 29886848 | tf_op jit(solution)/shard_map/jit(_take)/select_n | solution.py:30
  214.6 110.6 %all-reduce.9.cloned.1.call-done = f32[1024,2304]{1,0:T(8,128)} async-done(((f32[1024,2304]{1,0:T(8,128)}), f32[1024,2304]{1,0:T(8,128)}) %all-reduce.9.cloned.1.call-update) | async-done | bytes 9437200 | tf_op jit(solution)/shard_map/psum | solution.py:113
  325.2 7.7 all-to-all-start.1
  333.1 12.3 %scatter_custom_fusion.2 = s32[512]{0:T(512)S(1)} fusion(s32[2432]{0:T(1024)S(1)} %fusion.105, s32[2432]{0:T(1024)S(1)} %iota.147, s32[]{:T(128)} %constant.120.clone.1), kind=kCustom, calls=%fused_computation.200 | custom fusion | bytes 2052 | tf_op jit(solution)/shard_map/scatter | solution.py:46
  345.5 253.6 %all-to-all-done.1 = f32[16,152,1536]{2,1,0:T(8,128)} async-done(((f32[16,152,1536]{2,1,0:T(8,128)}), f32[16,152,1536]{2,1,0:T(8,128)}, u32[]{:S(2)}, u32[]{:S(2)}) %all-to-all-start.1) | async-done | bytes 14942240 | tf_op jit(solution)/shard_map/all_to_all | solution.py:115
  599.1 10.0 %gather_fusion.1 = f32[512,1536]{1,0:T(8,128)} fusion(f32[2432,1536]{1,0:T(8,128)} %bitcast.84, s32[1024]{0:T(1024)S(1)} %pad_clamp_fusion.1), kind=kCustom, calls=%fused_computation.1 | custom fusion | bytes 6293504 | tf_op jit(solution)/shard_map/jit(_take)/gather | solution.py:48
  609.1 2.2 broadcast_select_fusion.1
  614.3 11.7 %custom-call.20 = f32[128,128]{1,0:T(8,128)S(1)} custom-call(f32[128,128]{1,0:T(8,128)S(1)} %slice.241), custom_call_target="Cholesky" | custom-call | tf_op jit(solution)/shard_map/cholesky/custom-call.1 | solution.py:72
  627.4 9.8 %custom-call.21 = f32[1,128,128]{1,2,0:T(8,128)S(1)} custom-call(f32[1,128,128]{2,1,0:T(8,128)S(1)} %fusion.84), custom_call_target="InvertDiagBlocksLowerTriangular" | custom-call | tf_op jit(solution)/shard_map/triangular_solve/custom-call.0 | solution.py:73
  639.8 3.1 fusion.7
  647.4 12.1 %custom-call.22 = f32[128,128]{1,0:T(8,128)S(1)} custom-call(f32[128,128]{1,0:T(8,128)S(1)} %slice.384), custom_call_target="Cholesky" | custom-call | tf_op jit(solution)/shard_map/cholesky/custom-call.1 | solution.py:72
  661.0 9.8 %custom-call.23 = f32[1,128,128]{1,2,0:T(8,128)S(1)} custom-call(f32[1,128,128]{2,1,0:T(8,128)S(1)} %fusion.85), custom_call_target="InvertDiagBlocksLowerTriangular" | custom-call | tf_op jit(solution)/shard_map/triangular_solve/custom-call.0 | solution.py:73
  672.8 2.7 fusion.11
  679.1 13.3 %custom-call.24 = f32[128,128]{1,0:T(8,128)} custom-call(f32[128,128]{1,0:T(8,128)} %slice.392), custom_call_target="Cholesky" | custom-call | tf_op jit(solution)/shard_map/cholesky/custom-call.1 | solution.py:72
  693.9 2.1 fusion.86
  696.0 11.3 %custom-call.25 = f32[1,128,128]{1,2,0:T(8,128)} custom-call(f32[1,128,128]{2,1,0:T(8,128)} %fusion.86), custom_call_target="InvertDiagBlocksLowerTriangular" | custom-call | tf_op jit(solution)/shard_map/triangular_solve/custom-call.0 | solution.py:73
  712.8 3.3 fusion.15
  719.2 12.5 %custom-call.26 = f32[128,128]{1,0:T(8,128)S(1)} custom-call(f32[128,128]{1,0:T(8,128)} %slice.401), custom_call_target="Cholesky" | custom-call | tf_op jit(solution)/shard_map/cholesky/custom-call.1 | solution.py:72
  733.8 10.8 %custom-call.27 = f32[1,128,128]{1,2,0:T(8,128)S(1)} custom-call(f32[1,128,128]{2,1,0:T(8,128)} %fusion.87), custom_call_target="InvertDiagBlocksLowerTriangular" | custom-call | tf_op jit(solution)/shard_map/triangular_solve/custom-call.0 | solution.py:73
  753.7 12.5 %custom-call.28 = f32[128,128]{1,0:T(8,128)S(1)} custom-call(f32[128,128]{1,0:T(8,128)} %slice.410), custom_call_target="Cholesky" | custom-call | tf_op jit(solution)/shard_map/cholesky/custom-call.1 | solution.py:72
  768.1 10.6 %custom-call.29 = f32[1,128,128]{1,2,0:T(8,128)S(1)} custom-call(f32[1,128,128]{2,1,0:T(8,128)} %fusion.88), custom_call_target="InvertDiagBlocksLowerTriangular" | custom-call | tf_op jit(solution)/shard_map/triangular_solve/custom-call.0 | solution.py:73
  786.3 13.6 %custom-call.30 = f32[128,128]{1,0:T(8,128)} custom-call(f32[128,128]{1,0:T(8,128)} %slice.419), custom_call_target="Cholesky" | custom-call | tf_op jit(solution)/shard_map/cholesky/custom-call.1 | solution.py:72
  801.4 2.1 fusion.89
  803.5 11.3 %custom-call.31 = f32[1,128,128]{1,2,0:T(8,128)} custom-call(f32[1,128,128]{2,1,0:T(8,128)} %fusion.89), custom_call_target="InvertDiagBlocksLowerTriangular" | custom-call | tf_op jit(solution)/shard_map/triangular_solve/custom-call.0 | solution.py:73
  824.3 12.5 %custom-call.32 = f32[128,128]{1,0:T(8,128)S(1)} custom-call(f32[128,128]{1,0:T(8,128)} %get-tuple-element.21), custom_call_target="Cholesky" | custom-call | tf_op jit(solution)/shard_map/cholesky/custom-call.1 | solution.py:72
  838.9 11.4 %custom-call.33 = f32[1,128,128]{1,2,0:T(8,128)} custom-call(f32[1,128,128]{2,1,0:T(8,128)} %fusion.90), custom_call_target="InvertDiagBlocksLowerTriangular" | custom-call | tf_op jit(solution)/shard_map/triangular_solve/custom-call.0 | solution.py:73
  859.5 13.2 %custom-call.34 = f32[128,128]{1,0:T(8,128)} custom-call(f32[128,128]{1,0:T(8,128)} %slice_subtract_fusion.14), custom_call_target="Cholesky" | custom-call | tf_op jit(solution)/shard_map/cholesky/custom-call.1 | solution.py:72
  874.3 2.2 fusion.91
  876.5 11.3 %custom-call.35 = f32[1,128,128]{1,2,0:T(8,128)} custom-call(f32[1,128,128]{2,1,0:T(8,128)} %fusion.91), custom_call_target="InvertDiagBlocksLowerTriangular" | custom-call | tf_op jit(solution)/shard_map/triangular_solve/custom-call.0 | solution.py:73
  895.8 13.9 %fusion = f32[1024,1536]{1,0:T(8,128)S(1)} fusion(f32[1024,1024]{1,0:T(8,128)S(1)} %maximum_dynamic-update-slice_fusion, f32[1024,2304]{1,0:T(8,128)} %all-reduce.9.cloned.1.call-done), kind=kOutput, calls=%fused_computation.7 | convolution fusion | flops 9663676416 | bytes 16777216 | tf_op jit(solution)/shard_map/dot_general | solution.py:56
  909.8 2.6 copy-done.5
  913.2 9.3 reduce_sum.29
  922.5 6.7 fusion.139
  929.2 7.2 convolution_subtract_fusion
  (227 shorter events, 90.2 us)
Async XLA Ops:
  7.2 139.7 %all-gather.5.cloned.1.call-start = ((), (), s32[]{:S(2)}) async-start(), calls=%async_computation.3 | async-start | bytes 18874368 | tf_op jit(solution)/shard_map/all_gather | solution.py:13
  59.4 265.7 %all-reduce.9.cloned.1.call-start = ((), (), s32[]{:S(2)}) async-start(), calls=%async_computation.2 | async-start | bytes 18874368 | tf_op jit(solution)/shard_map/psum | solution.py:113
  156.2 3.6 copy-start
  176.5 0.7 copy-start.36
  181.9 143.2 %all-to-all-start = ((s32[16,1,152]{2,1,0:T(1,128)}), s32[16,1,152]{2,1,0:T(1,128)S(1)}, u32[]{:S(2)}, u32[]{:S(2)}) async-start(s32[16,1,152]{2,1,0:T(1,128)} %all_to_all.9), calls=%async_computation | async-start | bytes 32768 | tf_op jit(solution)/shard_map/all_to_all | solution.py:105
  325.2 273.9 %all-to-all-start.1 = ((f32[16,152,1536]{2,1,0:T(8,128)}), f32[16,152,1536]{2,1,0:T(8,128)}, u32[]{:S(2)}, u32[]{:S(2)}) async-start(f32[16,152,1536]{2,1,0:T(8,128)} %broadcast_select_fusion), calls=%async_computation.1 | async-start | bytes 29884416 | tf_op jit(solution)/shard_map/all_to_all | solution.py:115
  332.9 580.3 %all-gather.7.cloned.1.call-start = ((), (), s32[]{:S(2)}) async-start(), calls=%async_computation.4 | async-start | bytes 18874368 | tf_op jit(solution)/shard_map/all_gather | solution.py:13
  642.9 1.5 copy-start.20
  644.6 26.6 %slice-start.1 = ((f32[896,128]{1,0:T(8,128)}), f32[128,128]{1,0:T(8,128)S(1)}, s32[]{:S(2)}) async-start(f32[896,128]{1,0:T(8,128)} %copy-done.20), calls=%async_computation.6 | async-start | bytes 131072 | tf_op jit(solution)/shard_map/slice | solution.py:74
  645.0 1.7 copy-start.1
  671.2 4.5 copy-start.26
  671.2 4.4 slice-start.2
  672.8 3.5 copy-start.19
  672.8 4.4 copy-start.2
  677.6 1.4 copy-start.3
  710.5 5.5 copy-start.15
  712.8 5.0 copy-start.4
  718.0 1.2 copy-start.7
  746.5 4.6 copy-start.28
  746.5 4.2 copy-start.8
  746.5 4.2 copy-start.14
  751.1 1.0 copy-start.11
  780.6 4.7 copy-start.31
  780.6 3.1 copy-start.12
  780.6 4.7 copy-start.13
  782.3 2.2 copy-start.21
  783.8 0.8 copy-start.18
  819.6 3.9 copy-start.22
  821.6 1.0 copy-start.10
  823.6 27.9 %copy-start.25 = (f32[256,256]{1,0:T(8,128)}, f32[256,256]{1,0:T(8,128)S(1)}, u32[]{:S(2)}) copy-start(f32[256,256]{1,0:T(8,128)S(1)} %slice_subtract_fusion.13) | copy-start | bytes 786436
  851.4 2.2 copy-start.33
  852.1 2.3 copy-start.35
  852.1 4.5 copy-start.29
  852.1 39.0 %slice-start = ((f32[128,896]{1,0:T(8,128)}), f32[128,128]{1,0:T(8,128)S(1)}, s32[]{:S(2)}) async-start(f32[128,896]{1,0:T(8,128)} %copy-done.19), calls=%async_computation.5 | async-start | bytes 131072 | tf_op jit(solution)/shard_map/slice | solution.py:78
  854.4 39.7 %slice-start.3 = ((f32[128,896]{1,0:T(8,128)}), f32[128,512]{1,0:T(8,128)S(1)}, s32[]{:S(2)}) async-start(f32[128,896]{1,0:T(8,128)} %copy-done.21), calls=%async_computation.8 | async-start | bytes 524288 | tf_op jit(solution)/shard_map/slice | solution.py:78
  855.9 0.8 copy-start.23
  857.3 0.8 copy-start.16
  891.0 4.0 slice-start.4
  891.0 4.0 copy-start.27
  891.0 4.1 slice-start.5
  891.0 4.1 copy-start.30
  891.0 4.1 copy-start.17
  891.0 4.1 copy-start.24
  891.1 4.1 copy-start.32
  891.1 4.7 copy-start.34
  895.8 13.9 %copy-start.9 = (f32[1024,1024]{1,0:T(8,128)}, f32[1024,1024]{1,0:T(8,128)S(1)}, u32[]{:S(2)}) copy-start(f32[1024,1024]{1,0:T(8,128)S(1)} %maximum_dynamic-update-slice_fusion) | copy-start | bytes 12582916
  909.8 2.7 copy-start.5
  922.5 6.7 copy-start.6
Sparse Core Ops, SparseCore 0:
  59.5 87.3 all-gather.4
  176.7 148.4 all-reduce.8
  612.9 87.0 all-gather.6
